TPU v7x, 256 devices: a whole 4x4x8 slice. The times are simulated.
256 devices in a mesh: seq: 32 (over x, y, core), tensor: 8 (over z).
Axes of the slice: x: 4, y: 4, z: 8, core: 2. Of those that a mesh axis runs over, the one named last changes fastest.
Arguments:
- tokens: bfloat16 [4, 4, 1600], replicated, may hold values from -6 to 6
- first_gain: float32 [1600], replicated, may hold values from 0.25 to 1.75
- first_shift: float32 [1600], replicated, may hold values from -3 to 3
- input_weight: bfloat16 [1600, 3, 2048], P(None, None, 'tensor'), may hold values from -0.15625 to 0.15625
- input_bias: float32 [3, 2048], P(None, 'tensor')
- output_weight: bfloat16 [2048, 1600], P('tensor'), may hold values from -0.125 to 0.125
- output_bias: float32 [1600], replicated, may hold values from -3 to 3
- second_gain: float32 [1600], replicated, may hold values from 0.25 to 1.75
- second_shift: float32 [1600], replicated, may hold values from -3 to 3
- expand_weight: bfloat16 [1600, 6400], P(None, 'tensor'), may hold values from -0.15625 to 0.15625
- expand_bias: float32 [6400], P('tensor'), may hold values from -3 to 3
- contract_weight: bfloat16 [6400, 1600], P('tensor'), may hold values from -0.078125 to 0.078125
- contract_bias: float32 [1600], replicated, may hold values from -3 to 3
- key_cache: bfloat16 [4, 16384, 2048], P(None, 'seq', 'tensor')
- value_cache: bfloat16 [4, 16384, 2048], P(None, 'seq', 'tensor'), may hold values from -6 to 6
- cache_fill: int32 [4, 32], replicated, may hold values from 0 to 508, as said below
- owner_shard: int32 [4, 4], replicated, may hold values from 0 to 31, as said below
Outputs:
- hidden_out: bfloat16 [4, 4, 1600], replicated
- new_keys: bfloat16 [4, 16384, 2048], P(None, 'seq', 'tensor')
- new_values: bfloat16 [4, 16384, 2048], P(None, 'seq', 'tensor')
Inputs may be any that keep to these rules, and one draw needn't show every extreme that they name: `cache_fill`: 1 request hold 506 to 508 entries on every shard; every other request holds 1 to 508 entries on one shard and none on the others. `owner_shard`: a request with entries on one shard only appends all its new tokens to that shard.
All inputs are finite; a program needn't handle non-finite values.
Results may differ from a plain program's by a relative error of at most 0.0046.
Values sent between devices are 32-bit elements; how exact they have to be, the bound alone decides.
A program may use at most 64 MiB of HBM per device.

v0:
```python
import math
import jax
import jax.numpy as jnp
from jax import lax
from jax.sharding import PartitionSpec as P

HEAD_DIM = 64


def layer_norm(values, gain, shift):
    center = values - jnp.mean(values, axis=-1, keepdims=True)
    spread = jnp.mean(center * center, axis=-1, keepdims=True)
    return center * lax.rsqrt(spread + 1e-05) * gain + shift


def widen_heads(per_head):
    return jnp.repeat(per_head, HEAD_DIM, axis=-1)


def attend(queries, key_rows, value_rows, live_count):
    rounds, requests, row_width = queries.shape
    head_count = row_width // HEAD_DIM
    slot_count = key_rows.shape[1]
    query_heads = queries.reshape(rounds, requests, head_count, HEAD_DIM)
    key_heads = key_rows.reshape(requests, slot_count, head_count, HEAD_DIM)
    value_heads = value_rows.reshape(requests, slot_count, head_count, HEAD_DIM)
    scores = jnp.einsum(
        "tbhd,bshd->tbhs", query_heads, key_heads, preferred_element_type=jnp.float32
    ) * (1.0 / math.sqrt(HEAD_DIM))
    usable = (lax.iota(jnp.int32, slot_count)[None, None, :] < live_count[:, :, None])[
        :, :, None, :
    ]
    peaks = jnp.max(jnp.where(usable, scores, -1e30), axis=-1)
    weights = jnp.where(usable, jnp.exp(scores - peaks[..., None]), 0.0)
    totals = jnp.sum(weights, axis=-1)
    blended = jnp.einsum(
        "tbhs,bshd->tbhd",
        weights.astype(jnp.bfloat16),
        value_heads,
        preferred_element_type=jnp.float32,
    )
    return (peaks, totals, blended.reshape(rounds, requests, row_width))


def merge_heads(parts):
    peaks, totals, blended = parts
    highest = lax.pmax(peaks, "seq")
    factor = jnp.exp(peaks - highest)
    totals, blended = lax.psum((totals * factor, blended * widen_heads(factor)), "seq")
    return (blended / widen_heads(totals)).astype(jnp.bfloat16)


def project_in(rows, first_gain, first_shift, input_weight, input_bias):
    normed = layer_norm(rows.astype(jnp.float32), first_gain, first_shift).astype(jnp.bfloat16)
    packed = (
        jnp.einsum("rd,dch->rch", normed, input_weight, preferred_element_type=jnp.float32)
        + input_bias
    )
    return packed.astype(jnp.bfloat16)


def finish(
    rows,
    attended,
    output_weight,
    output_bias,
    second_gain,
    second_shift,
    expand_weight,
    expand_bias,
    contract_weight,
    contract_bias,
):
    heads_sum = lax.psum(
        jnp.dot(attended, output_weight, preferred_element_type=jnp.float32), "tensor"
    )
    middle = rows.astype(jnp.float32) + heads_sum + output_bias
    second = layer_norm(middle, second_gain, second_shift).astype(jnp.bfloat16)
    hidden = jax.nn.gelu(
        jnp.dot(second, expand_weight, preferred_element_type=jnp.float32) + expand_bias,
        approximate=True,
    ).astype(jnp.bfloat16)
    units_sum = lax.psum(
        jnp.dot(hidden, contract_weight, preferred_element_type=jnp.float32), "tensor"
    )
    return (units_sum + contract_bias + middle).astype(jnp.bfloat16)


def write_cache(cache, fresh_rows, slot_index, owned):
    slot_count = cache.shape[1]
    places = (lax.iota(jnp.int32, slot_count)[None, :] == slot_index[:, None]) & (
        owned[:, None] > 0
    )
    return jnp.where(places[:, :, None], fresh_rows[:, None, :], cache)


def per_device(
    tokens,
    first_gain,
    first_shift,
    input_weight,
    input_bias,
    output_weight,
    output_bias,
    second_gain,
    second_shift,
    expand_weight,
    expand_bias,
    contract_weight,
    contract_bias,
    key_cache,
    value_cache,
    cache_fill,
    owner_shard,
):
    shard = lax.axis_index("seq")
    shard_count = cache_fill.shape[1]
    picked = lax.iota(jnp.int32, shard_count)[None, :] == shard
    own_fill = jnp.sum(jnp.where(picked, cache_fill, 0), axis=1)
    owned = (owner_shard == shard).astype(jnp.int32)
    through = jnp.cumsum(owned, axis=0)
    slot_index = own_fill[None, :] + through - owned
    live_count = own_fill[None, :] + through
    step_total, requests, model_width = tokens.shape
    outputs = []
    for step_index in range(step_total):
        packed = project_in(tokens[step_index], first_gain, first_shift, input_weight, input_bias)
        key_cache = write_cache(key_cache, packed[:, 1], slot_index[step_index], owned[step_index])
        value_cache = write_cache(
            value_cache, packed[:, 2], slot_index[step_index], owned[step_index]
        )
        parts = attend(
            packed[None, :, 0], key_cache, value_cache, live_count[step_index : step_index + 1]
        )
        attended = merge_heads(parts)[0]
        outputs.append(
            finish(
                tokens[step_index],
                attended,
                output_weight,
                output_bias,
                second_gain,
                second_shift,
                expand_weight,
                expand_bias,
                contract_weight,
                contract_bias,
            )
        )
    hidden_out = jnp.stack(outputs)
    return (hidden_out, key_cache, value_cache)


def solution(mesh):
    return jax.shard_map(
        per_device,
        mesh=mesh,
        in_specs=(
            P(),
            P(),
            P(),
            P(None, None, "tensor"),
            P(None, "tensor"),
            P("tensor", None),
            P(),
            P(),
            P(),
            P(None, "tensor"),
            P("tensor"),
            P("tensor", None),
            P(),
            P(None, "seq", "tensor"),
            P(None, "seq", "tensor"),
            P(),
            P(),
        ),
        out_specs=(P(), P(None, "seq", "tensor"), P(None, "seq", "tensor")),
        check_vma=False,
    )
```

profile of v0, /device:TPU:2, one launch (start us, length us, event | category | flops | bytes accessed | tf_op | source)
XLA Modules:
  0.0 433.3 jit_solution(10217517019822369008)
XLA Ops:
  10.3 2.2 fusion.3
  13.5 2.3 copy.25
  15.8 2.2 fusion
  18.0 2.3 copy.24
  20.9 4.8 %broadcast_select_fusion = (bf16[4,512,256]{1,2,0:T(8,128)(2,1)S(1)}, bf16[4,512,256]{1,2,0:T(8,128)(2,1)}, bf16[4,512,256]{1,2,0:T(8,128)(2,1)}, bf16[4,512,256...) fusion(pred[4,512]{1,0:T(4,128)(4,1)S(1)} %fusion.151, ...), kind=kLoop, calls=%fused_computation.12 | loop fusion | flops 4194304 | bytes 10510336 | tf_op jit(solution)/shard_map/jit(_where)/select_n | solution.py:94
  28.2 1.5 fusion.223
  31.2 1.5 fusion.222
  34.0 1.5 fusion.221
  37.8 57.0 %all-reduce.1 = (f32[1,4,4]{2,1,0:T(4,128)}, f32[1,4,4]{2,1,0:T(4,128)}, f32[1,4,4]{2,1,0:T(4,128)}, f32[1,4,4]{2,1,0:T(4,128)}) all-reduce(f32[1,4,4]{2,1,0:T(4,128)S(1)} %bitcast.321, f32[1,4,4]{2,1,0:T(4,128)S(1)} %bitcast.323, f32[1,4,4]{2,1,0:T(4,128)S(1)} %bitcast.322, ...), channel_id=1, replica_groups=mesh['seq'=32,'tensor'=8] {'seq'}, use_global_device_ids=true, to_apply=%region_38.39 | all-reduce | flops 64 | bytes 512 | tf_op jit(solution)/shard_map/pmax | solution.py:47
  97.4 1.4 mul.328
  98.8 1.6 fusion.14
  102.4 1.6 fusion.16
  106.0 1.4 mul.296
  107.4 1.6 fusion.18
  111.0 1.4 mul.279
  112.4 118.0 %all-reduce = (f32[1,4,256]{2,1,0:T(4,128)}, f32[4,4]{1,0:T(4,128)}, f32[1,4,256]{2,1,0:T(4,128)}, f32[4,4]{1,0:T(4,128)}, f32[1,4,256]{2,1,0:T(4,128)}, /*index...) all-reduce(f32[1,4,256]{2,1,0:T(4,128)} %mul.328, ...), channel_id=1, replica_groups=mesh['seq'=32,'tensor'=8] {'seq'}, use_global_device_ids=true, to_apply=%region_39.40 | all-reduce | flops 4160 | bytes 33280 | tf_op jit(solution)/shard_map/psum | solution.py:49
  231.7 1.4 broadcast_in_dim.308
  234.4 1.4 broadcast_in_dim.299
  237.1 1.4 broadcast_in_dim.290
  239.8 1.4 broadcast_in_dim.281
  241.2 1.6 fusion.176
  242.8 1.6 fusion.179
  244.5 1.6 fusion.182
  246.1 1.6 fusion.185
  247.8 88.4 %all-reduce.9.cloned.1.call-done = (f32[4,1600]{1,0:T(4,128)}, f32[4,1600]{1,0:T(4,128)}, f32[4,1600]{1,0:T(4,128)}, f32[4,1600]{1,0:T(4,128)}) async-done(((f32[4,1600]{1,0:T(4,128)}, f32[4,1600]{1,0:T(4,128)}, f32[4,1600]{1,0:T(4,128)}, f32[4,1600]{1,0:T(4,128)}), (f32[4,1600]{1,0:T(4,128)}, f32[4,1600]{1,0:T(4,128)}, f32[4,1600]{1,0:T(4,128)}, f32[4,1600]{1,0:T(4,128)})) %all-reduce.9.cloned.1.call-update) | async-done | bytes 102416 | tf_op jit(solution)/shard_map/psum | solution.py:74
  337.7 3.9 fusion.83
  341.6 3.9 fusion.74
  345.7 3.9 fusion.65
  349.8 3.9 fusion.56
  353.8 2.3 copy.26
  356.0 2.3 copy.27
  358.3 66.6 %all-reduce.7.cloned.1.call-done = (f32[4,1600]{1,0:T(4,128)}, f32[4,1600]{1,0:T(4,128)}, f32[4,1600]{1,0:T(4,128)}, f32[4,1600]{1,0:T(4,128)}) async-done(((f32[4,1600]{1,0:T(4,128)}, f32[4,1600]{1,0:T(4,128)}, f32[4,1600]{1,0:T(4,128)}, f32[4,1600]{1,0:T(4,128)}), (f32[4,1600]{1,0:T(4,128)}, f32[4,1600]{1,0:T(4,128)}, f32[4,1600]{1,0:T(4,128)}, f32[4,1600]{1,0:T(4,128)})) %all-reduce.7.cloned.1.call-update) | async-done | bytes 102416 | tf_op jit(solution)/shard_map/psum | solution.py:83
  (111 shorter events, 29.8 us)
Async XLA Ops:
  7.2 330.4 %copy-start = (bf16[800,1600]{1,0:T(8,128)(2,1)S(1)}, bf16[800,1600]{1,0:T(8,128)(2,1)}, u32[]{:S(2)}) copy-start(bf16[800,1600]{1,0:T(8,128)(2,1)} %param.28) | copy-start | bytes 7680004
  7.2 5.3 %copy-start.5 = (bf16[4,4,1600]{2,1,0:T(4,128)(2,1)S(1)}, bf16[4,4,1600]{2,1,0:T(4,128)(2,1)}, u32[]{:S(2)}) copy-start(bf16[4,4,1600]{2,1,0:T(4,128)(2,1)} %param.17) | copy-start | bytes 153604
  7.2 5.3 %copy-start.6 = (f32[1600]{0:T(1024)S(1)}, f32[1600]{0:T(1024)}, u32[]{:S(2)}) copy-start(f32[1600]{0:T(1024)} %param.19) | copy-start | bytes 19204
  7.2 5.3 %copy-start.7 = (f32[1600]{0:T(1024)S(1)}, f32[1600]{0:T(1024)}, u32[]{:S(2)}) copy-start(f32[1600]{0:T(1024)} %param.18) | copy-start | bytes 19204
  7.2 5.3 %copy-start.10 = (f32[3,256]{1,0:T(4,128)S(1)}, f32[3,256]{1,0:T(4,128)}, u32[]{:S(2)}) copy-start(f32[3,256]{1,0:T(4,128)} %param.21) | copy-start | bytes 9220
  7.2 329.0 %all-reduce.9.cloned.1.call-start = ((), (), s32[]{:S(2)}) async-start(), calls=%async_computation.1 | async-start | bytes 212992 | tf_op jit(solution)/shard_map/psum | solution.py:74
  8.2 4.4 %copy-start.1 = (bf16[1600,3,256]{2,0,1:T(8,128)(2,1)S(1)}, bf16[1600,3,256]{2,0,1:T(8,128)(2,1)}, u32[]{:S(2)}) copy-start(bf16[1600,3,256]{2,0,1:T(8,128)(2,1)} %param.20) | copy-start | bytes 7372804
  15.8 4.6 %copy-start.17 = (s32[4,32]{1,0:T(4,128)S(1)}, s32[4,32]{1,0:T(4,128)}, u32[]{:S(2)}) copy-start(s32[4,32]{1,0:T(4,128)} %param.32) | copy-start | bytes 1540
  15.8 4.7 %copy-start.16 = (s32[4,4]{1,0:T(4,128)S(1)}, s32[4,4]{1,0:T(4,128)}, u32[]{:S(2)}) copy-start(s32[4,4]{1,0:T(4,128)} %param.33) | copy-start | bytes 196
  25.7 1.0 copy-start.3
  28.2 8.7 %copy-start.4 = (bf16[4,512,256]{1,2,0:T(8,128)(2,1)S(1)}, bf16[4,512,256]{1,2,0:T(8,128)(2,1)}, u32[]{:S(2)}) copy-start(bf16[4,512,256]{1,2,0:T(8,128)(2,1)} %get-tuple-element.73) | copy-start | bytes 3145732
  28.2 8.7 %copy-start.14 = (bf16[4,4,512,1]{2,1,0,3:T(4,128)(2,1)S(1)}, bf16[4,4,512,1]{2,1,0,3:T(4,128)(2,1)}, u32[]{:S(2)}) copy-start(bf16[4,4,512,1]{2,1,0,3:T(4,128)(2,1)} %get-tuple-element.68) | copy-start | bytes 49156
  32.7 69.7 %copy-start.13 = (f32[4,4]{1,0:T(4,128)}, f32[4,4]{1,0:T(4,128)S(1)}, u32[]{:S(2)}) copy-start(f32[4,4]{1,0:T(4,128)S(1)} %select_reduce_fusion.2) | copy-start | bytes 196
  35.5 205.7 %copy-start.2 = (bf16[256,1600]{0,1:T(8,128)(2,1)S(1)}, bf16[256,1600]{0,1:T(8,128)(2,1)}, u32[]{:S(2)}) copy-start(bf16[256,1600]{0,1:T(8,128)(2,1)} %param.22) | copy-start | bytes 2457604
  35.6 66.9 %copy-start.12 = (f32[4,4]{1,0:T(4,128)}, f32[4,4]{1,0:T(4,128)S(1)}, u32[]{:S(2)}) copy-start(f32[4,4]{1,0:T(4,128)S(1)} %select_reduce_fusion.3) | copy-start | bytes 196
  104.0 233.6 %copy-start.8 = (f32[1600]{0:T(1024)S(1)}, f32[1600]{0:T(1024)}, u32[]{:S(2)}) copy-start(f32[1600]{0:T(1024)} %param.25) | copy-start | bytes 19204
  104.0 233.6 %copy-start.9 = (f32[1600]{0:T(1024)S(1)}, f32[1600]{0:T(1024)}, u32[]{:S(2)}) copy-start(f32[1600]{0:T(1024)} %param.24) | copy-start | bytes 19204
  104.0 233.6 %copy-start.11 = (f32[800]{0:T(1024)S(1)}, f32[800]{0:T(1024)}, u32[]{:S(2)}) copy-start(f32[800]{0:T(1024)} %param.27) | copy-start | bytes 9604
  247.7 177.2 %all-reduce.7.cloned.1.call-start = ((), (), s32[]{:S(2)}) async-start(), calls=%async_computation | async-start | bytes 212992 | tf_op jit(solution)/shard_map/psum | solution.py:83
  353.8 71.2 %copy-start.15 = (f32[1600]{0:T(1024)S(1)}, f32[1600]{0:T(1024)}, u32[]{:S(2)}) copy-start(f32[1600]{0:T(1024)} %param.29) | copy-start | bytes 19204
Sparse Core Ops, SparseCore 0:
  247.9 88.2 all-reduce.8
  353.9 70.9 all-reduce.6
where the time goes:
time: 435 us; the launch traced here: 433 us
  blocking collectives  175 us (40%)
  waiting for transfers between devices  155 us (36%)
  matrix products  38 us (9%)
  local copies, waits for them, and re-layouts  26.2 us (6%)
  other arithmetic  24.7 us (6%)
  between operations  14.3 us (3%)
    psum x1, blocking collectives, merge_heads(): lax.psum((totals * factor, blended * widen_heads(factor)), 'seq')  118 us
    psum x1, waiting for transfers between devices, finish(): lax.psum(jnp.dot(attended, output_weight, preferred_element_type=jnp.floa...  88.4 us
    psum x1, waiting for transfers between devices, finish(): lax.psum(jnp.dot(hidden, contract_weight, preferred_element_type=jnp.floa...  66.6 us
    pmax x1, blocking collectives, merge_heads(): highest = lax.pmax(peaks, 'seq')  57 us
    dot_general x4, matrix products, finish(): jnp.dot(hidden, contract_weight, preferred_element_type=jnp.float32)  15.7 us
    broadcast_in_dim x8, local copies, waits for them, and re-layouts, widen_heads(): return jnp.repeat(per_head, HEAD_DIM, axis=-1)  10.9 us
    unnamed x40, local copies, waits for them, and re-layouts  10.2 us
  transfers between devices with their start and end apart: 2, of which 2 were waited for; matrix products, arithmetic and copies ran while one was open for 1% of the time, Pallas kernels for 0%

commit v1 on v0

--- a/solution.py
+++ b/solution.py
@@ -71,8 +71,11 @@
     contract_weight,
     contract_bias,
 ):
-    heads_sum = lax.psum(
-        jnp.dot(attended, output_weight, preferred_element_type=jnp.float32), "tensor"
+    heads_sum = jnp.sum(
+        lax.all_gather(
+            jnp.dot(attended, output_weight, preferred_element_type=jnp.float32), "tensor"
+        ),
+        axis=0,
     )
     middle = rows.astype(jnp.float32) + heads_sum + output_bias
     second = layer_norm(middle, second_gain, second_shift).astype(jnp.bfloat16)

time: 435 us -> 462 us (1.062)
  blocking collectives: 175 us -> 284 us
  waiting for transfers between devices: 155 us -> 80.3 us
  local copies, waits for them, and re-layouts: 26.2 us -> 20.7 us
    all_gather x0 -> x4, blocking collectives: none -> 109 us  [finish(): lax.all_gather(jnp.dot(attended, output_weight, preferred_element_type=jn...]
    psum x1 -> x0, waiting for transfers between devices: 88.4 us -> none  [finish(): lax.psum(jnp.dot(attended, output_weight, preferred_element_type=jnp.floa...]
    psum x1, waiting for transfers between devices: 66.6 us -> 80.3 us  [finish(): lax.psum(jnp.dot(hidden, contract_weight, preferred_element_type=jnp.floa...]
    reduce_sum x0 -> x4, other arithmetic: none -> 4.79 us  [finish(): jnp.sum(lax.all_gather(jnp.dot(attended, output_weight, preferred_element...]
    unnamed x40 -> x30, local copies, waits for them, and re-layouts: 10.2 us -> 9.14 us
  transfers between devices with their start and end apart: 2 -> 1, of which waited for: 2 -> 1; matrix products, arithmetic and copies ran while one was open for 1% -> 1% of each run, Pallas kernels for 0% -> 0%
where the time goes in v1:
time: 462 us; the launch traced here: 460 us
  blocking collectives  284 us (61%)
  waiting for transfers between devices  80.3 us (17%)
  matrix products  35 us (8%)
  other arithmetic  26.2 us (6%)
  local copies, waits for them, and re-layouts  20.7 us (4%)
  between operations  14.3 us (3%)
    psum x1, blocking collectives, merge_heads(): lax.psum((totals * factor, blended * widen_heads(factor)), 'seq')  118 us
    all_gather x4, blocking collectives, finish(): lax.all_gather(jnp.dot(attended, output_weight, preferred_element_type=jn...  109 us
    psum x1, waiting for transfers between devices, finish(): lax.psum(jnp.dot(hidden, contract_weight, preferred_element_type=jnp.floa...  80.3 us
    pmax x1, blocking collectives, merge_heads(): highest = lax.pmax(peaks, 'seq')  57 us
    dot_general x4, matrix products, finish(): jnp.dot(hidden, contract_weight, preferred_element_type=jnp.float32)  15.7 us
  transfers between devices with their start and end apart: 1, of which 1 were waited for; matrix products, arithmetic and copies ran while one was open for 1% of the time, Pallas kernels for 0%

profile of v1, /device:TPU:2, one launch (start us, length us, event | category | flops | bytes accessed | tf_op | source)
XLA Modules:
  0.0 460.4 jit_solution(12109323459616348327)
XLA Ops:
  9.5 2.2 fusion
  14.1 2.3 copy.28
  16.4 2.3 copy.29
  19.3 4.8 %broadcast_select_fusion = (bf16[4,512,256]{1,2,0:T(8,128)(2,1)}, bf16[4,512,256]{1,2,0:T(8,128)(2,1)}, bf16[4,512,256]{1,2,0:T(8,128)(2,1)}, bf16[4,512,256]{1,...) fusion(pred[4,512]{1,0:T(4,128)(4,1)S(1)} %fusion.151, ...), kind=kLoop, calls=%fused_computation.16 | loop fusion | flops 4194304 | bytes 10510336 | tf_op jit(solution)/shard_map/jit(_where)/select_n | solution.py:97
  25.5 1.5 fusion.218
  28.4 1.5 fusion.219
  31.2 1.5 fusion.220
  34.1 57.0 %all-reduce.1 = (f32[1,4,4]{2,1,0:T(4,128)}, f32[1,4,4]{2,1,0:T(4,128)}, f32[1,4,4]{2,1,0:T(4,128)}, f32[1,4,4]{2,1,0:T(4,128)}) all-reduce(f32[1,4,4]{2,1,0:T(4,128)S(1)} %bitcast.328, f32[1,4,4]{2,1,0:T(4,128)S(1)} %bitcast.330, f32[1,4,4]{2,1,0:T(4,128)S(1)} %bitcast.331, ...), channel_id=1, replica_groups=mesh['seq'=32,'tensor'=8] {'seq'}, use_global_device_ids=true, to_apply=%region_38.39 | all-reduce | flops 64 | bytes 512 | tf_op jit(solution)/shard_map/pmax | solution.py:47
  92.3 1.6 fusion.18
  94.6 1.4 mul.279
  97.2 1.6 fusion.16
  100.3 1.6 fusion.14
  103.3 1.6 fusion.12
  105.1 118.0 %all-reduce = (f32[1,4,256]{2,1,0:T(4,128)}, f32[4,4]{1,0:T(4,128)}, f32[1,4,256]{2,1,0:T(4,128)}, f32[4,4]{1,0:T(4,128)}, f32[1,4,256]{2,1,0:T(4,128)}, /*index...) all-reduce(f32[1,4,256]{2,1,0:T(4,128)S(1)} %mul.328, ...), channel_id=1, replica_groups=mesh['seq'=32,'tensor'=8] {'seq'}, use_global_device_ids=true, to_apply=%region_39.40 | all-reduce | flops 4160 | bytes 33280 | tf_op jit(solution)/shard_map/psum | solution.py:49
  224.9 30.5 %all-gather.7 = f32[8,4,1600]{2,1,0:T(4,128)} all-gather(f32[1,4,1600]{2,1,0:T(4,128)S(1)} %convolution_bitcast_fusion), channel_id=5, replica_groups=mesh['seq'=32,'tensor'=8] {'tensor'}, dimensions={0}, use_global_device_ids=true | all-gather | bytes 230400 | tf_op jit(solution)/shard_map/all_gather | solution.py:75
  255.5 1.3 broadcast_in_dim.298
  256.8 1.4 broadcast_in_dim.299
  259.2 26.7 %all-gather.6 = f32[8,4,1600]{2,1,0:T(4,128)} all-gather(f32[1,4,1600]{2,1,0:T(4,128)S(1)} %convolution_bitcast_fusion.1), channel_id=4, replica_groups=mesh['seq'=32,'tensor'=8] {'tensor'}, dimensions={0}, use_global_device_ids=true | all-gather | bytes 230400 | tf_op jit(solution)/shard_map/all_gather | solution.py:75
  285.9 1.6 reduce_sum.259
  287.5 1.6 reduce_sum.252
  290.4 1.4 broadcast_in_dim.290
  292.8 26.8 %all-gather.5 = f32[8,4,1600]{2,1,0:T(4,128)} all-gather(f32[1,4,1600]{2,1,0:T(4,128)S(1)} %convolution_bitcast_fusion.2), channel_id=3, replica_groups=mesh['seq'=32,'tensor'=8] {'tensor'}, dimensions={0}, use_global_device_ids=true | all-gather | bytes 230400 | tf_op jit(solution)/shard_map/all_gather | solution.py:75
  319.6 1.6 reduce_sum.245
  322.5 1.4 broadcast_in_dim.281
  324.8 24.7 %all-gather.4 = f32[8,4,1600]{2,1,0:T(4,128)S(1)} all-gather(f32[1,4,1600]{2,1,0:T(4,128)S(1)} %convolution_bitcast_fusion.3), channel_id=2, replica_groups=mesh['seq'=32,'tensor'=8] {'tensor'}, dimensions={0}, use_global_device_ids=true | all-gather | bytes 230400 | tf_op jit(solution)/shard_map/all_gather | solution.py:75
  351.1 3.9 fusion.56
  355.0 3.9 fusion.65
  359.1 3.9 fusion.74
  363.2 3.9 fusion.83
  367.2 2.3 copy.30
  369.4 2.3 copy.31
  371.7 80.3 %all-reduce.5.cloned.1.call-done = (f32[4,1600]{1,0:T(4,128)}, f32[4,1600]{1,0:T(4,128)}, f32[4,1600]{1,0:T(4,128)}, f32[4,1600]{1,0:T(4,128)}) async-done(((f32[4,1600]{1,0:T(4,128)}, f32[4,1600]{1,0:T(4,128)}, f32[4,1600]{1,0:T(4,128)}, f32[4,1600]{1,0:T(4,128)}), (f32[4,1600]{1,0:T(4,128)}, f32[4,1600]{1,0:T(4,128)}, f32[4,1600]{1,0:T(4,128)}, f32[4,1600]{1,0:T(4,128)})) %all-reduce.5.cloned.1.call-update) | async-done | bytes 102416 | tf_op jit(solution)/shard_map/psum | solution.py:86
  (106 shorter events, 27.9 us)
Async XLA Ops:
  7.2 343.8 %copy-start = (bf16[800,1600]{1,0:T(8,128)(2,1)S(1)}, bf16[800,1600]{1,0:T(8,128)(2,1)}, u32[]{:S(2)}) copy-start(bf16[800,1600]{1,0:T(8,128)(2,1)} %param.28) | copy-start | bytes 7680004
  7.2 5.8 %copy-start.3 = (bf16[4,4,1600]{2,1,0:T(4,128)(2,1)S(1)}, bf16[4,4,1600]{2,1,0:T(4,128)(2,1)}, u32[]{:S(2)}) copy-start(bf16[4,4,1600]{2,1,0:T(4,128)(2,1)} %param.17) | copy-start | bytes 153604
  7.2 5.8 %copy-start.5 = (f32[1600]{0:T(1024)S(1)}, f32[1600]{0:T(1024)}, u32[]{:S(2)}) copy-start(f32[1600]{0:T(1024)} %param.18) | copy-start | bytes 19204
  7.2 5.8 %copy-start.4 = (f32[1600]{0:T(1024)S(1)}, f32[1600]{0:T(1024)}, u32[]{:S(2)}) copy-start(f32[1600]{0:T(1024)} %param.19) | copy-start | bytes 19204
  7.2 5.8 %copy-start.8 = (f32[3,256]{1,0:T(4,128)S(1)}, f32[3,256]{1,0:T(4,128)}, u32[]{:S(2)}) copy-start(f32[3,256]{1,0:T(4,128)} %param.21) | copy-start | bytes 9220
  7.2 444.8 %all-reduce.5.cloned.1.call-start = ((), (), s32[]{:S(2)}) async-start(), calls=%async_computation | async-start | bytes 212992 | tf_op jit(solution)/shard_map/psum | solution.py:86
  7.3 4.5 copy-start.1
  13.0 1.1 copy-start.11
  14.0 4.7 %copy-start.12 = (s32[4,32]{1,0:T(4,128)S(1)}, s32[4,32]{1,0:T(4,128)}, u32[]{:S(2)}) copy-start(s32[4,32]{1,0:T(4,128)} %param.32) | copy-start | bytes 1540
  32.7 191.2 %copy-start.2 = (bf16[256,1600]{0,1:T(8,128)(2,1)S(1)}, bf16[256,1600]{0,1:T(8,128)(2,1)}, u32[]{:S(2)}) copy-start(bf16[256,1600]{0,1:T(8,128)(2,1)} %param.22) | copy-start | bytes 2457604
  224.9 126.1 %copy-start.6 = (f32[1600]{0:T(1024)S(1)}, f32[1600]{0:T(1024)}, u32[]{:S(2)}) copy-start(f32[1600]{0:T(1024)} %param.25) | copy-start | bytes 19204
  224.9 126.1 %copy-start.7 = (f32[1600]{0:T(1024)S(1)}, f32[1600]{0:T(1024)}, u32[]{:S(2)}) copy-start(f32[1600]{0:T(1024)} %param.24) | copy-start | bytes 19204
  224.9 126.1 %copy-start.9 = (f32[800]{0:T(1024)S(1)}, f32[800]{0:T(1024)}, u32[]{:S(2)}) copy-start(f32[800]{0:T(1024)} %param.27) | copy-start | bytes 9604
  367.1 84.9 %copy-start.10 = (f32[1600]{0:T(1024)S(1)}, f32[1600]{0:T(1024)}, u32[]{:S(2)}) copy-start(f32[1600]{0:T(1024)} %param.29) | copy-start | bytes 19204
Sparse Core Ops, SparseCore 0:
  367.3 84.6 all-reduce.4
